TPU v7x, 32 devices: a whole 2x2x4 slice. The times are simulated.
32 devices in a mesh: parts: 2 (over y), row: 4 (over z), col: 4 (over x, core).
Axes of the slice: x: 2, y: 2, z: 4, core: 2. Of those that a mesh axis runs over, the one named last changes fastest.
Arguments:
- sigma_anc: float32 [24576, 12288], P(('parts', 'row'), 'col'), parts along dimension 0
- normal_factor: float32 [4, 12288, 512], P('parts', ('col', 'row')), parts along dimension 0, may hold values from -0.078125 to 0.078125
- jj_inverse: float32 [4, 512, 512], P('parts', None, 'col'), parts along dimension 0, may hold values from -6 to 6
- blocks: int32 [4, 128], P('parts'), parts along dimension 0, may hold values from 0 to 255, as said below
Outputs:
- sigma_rj: float32 [4, 12288, 512], P('parts', 'row', 'col'), parts along dimension 0
- sigma_jj: float32 [4, 512, 512], P('parts', None, 'col'), parts along dimension 0
There are 2 independent parts, one for each index of `parts`. A program takes and returns all parts, laid end to end along the dimension named above; each array names one. Nothing has to cross between parts.
Inputs may be any that keep to these rules, and one draw needn't show every extreme that they name: Each list names 128 different blocks and always holds block 0 and block 255.
All inputs are finite; a program needn't handle non-finite values.
Results may differ from a plain program's by a relative error of at most 0.0001.
Values sent between devices are 32-bit elements; how exact they have to be, the bound alone decides.
A program may use at most 192 MiB of HBM per device.

v0:
```python
import jax
import jax.numpy as jnp
from jax import lax
from jax.sharding import PartitionSpec as P

BLK = 48


def listed_mask(blocks, first_block, count, rows):
    block_ids = first_block + jnp.arange(count, dtype=jnp.int32)
    listed = jnp.any(blocks[:, :, None] == block_ids[None, None, :], axis=1).astype(jnp.float32)
    return jnp.repeat(listed, BLK, axis=1, total_repeat_length=rows)[:, :, None]


def shards(sigma_anc, normal_factor, jj_inverse, blocks):
    tile_rows, tile_cols = sigma_anc.shape
    row_count = lax.axis_size("row")
    row_index = lax.axis_index("row")
    col_index = lax.axis_index("col")
    local_rows = normal_factor.shape[1]
    local_blocks = local_rows // BLK
    first_local = (col_index * row_count + row_index) * local_blocks
    masked = normal_factor * listed_mask(blocks, first_local, local_blocks, local_rows)
    row_blocks = tile_rows // BLK
    row_mask = listed_mask(blocks, row_index * row_blocks, row_blocks, tile_rows)
    start_row = row_index * tile_rows
    root_col = start_row // tile_cols
    offset = jnp.clip(start_row - col_index * tile_cols, 0, tile_cols - tile_rows)
    is_root = (col_index == root_col).astype(jnp.float32)
    rj_list = []
    update_list = []
    for supernode in range(2):
        gathered = lax.all_gather(masked[supernode], "row", axis=0, tiled=True)
        partial = jnp.dot(
            sigma_anc, gathered, precision=lax.Precision.HIGH, preferred_element_type=jnp.float32
        )
        own_rj = -lax.psum_scatter(
            partial * row_mask[supernode], "col", scatter_dimension=1, tiled=True
        )
        rj_list.append(own_rj)
        wide_rj = lax.all_gather(own_rj, "col", axis=1, tiled=True)
        slab = lax.dynamic_slice_in_dim(gathered, offset, tile_rows, 0) * is_root
        update = lax.dot_general(
            slab,
            wide_rj,
            (((0,), (0,)), ((), ())),
            precision=lax.Precision.HIGH,
            preferred_element_type=jnp.float32,
        )
        update_list.append(
            lax.psum(lax.psum_scatter(update, "col", scatter_dimension=1, tiled=True), "row")
        )
    return (jnp.stack(rj_list), jj_inverse - jnp.stack(update_list))


def solution(mesh):
    placed = (
        P(("parts", "row"), "col"),
        P("parts", ("col", "row"), None),
        P("parts", None, "col"),
        P("parts", None),
    )
    return jax.shard_map(
        shards,
        mesh=mesh,
        in_specs=placed,
        out_specs=(P("parts", "row", "col"), P("parts", None, "col")),
        check_vma=False,
    )
```

profile of v0, /device:TPU:0, one launch (start us, length us, event | category | flops | bytes accessed | tf_op | source)
XLA Modules:
  0.0 573.0 jit_solution(10979280178893593499)
XLA Ops:
  7.2 0.9 compare_reduce_fusion.1
  8.1 0.1 copy.10
  8.2 0.7 pad_clamp_fusion
  8.9 1.6 gather_fusion
  10.5 0.1 copy.11
  10.6 2.2 broadcast_multiply_fusion
  12.8 2.0 fusion.12
  14.9 0.7 all-gather.13.cloned.1.call-update
  15.6 0.2 compare_reduce_fusion
  15.8 0.1 copy.12
  15.9 8.1 %gather_fusion.1 = f32[3072,2]{1,0:T(8,128)S(1)} fusion(f32[2,64]{0,1:T(8,128)S(1)} %copy.12, s32[3072]{0:T(1024)S(1)} %broadcast_clamp_fusion), kind=kCustom, calls=%fused_computation.1 | custom fusion | bytes 61440 | tf_op jit(solution)/shard_map/jit(_take)/gather | solution.py:12
  24.1 1.3 slice_reduce_fusion.1
  25.4 107.6 %all-gather.11.cloned.1.call-done = f32[1,3072,512]{2,1,0:T(8,128)} async-done(((f32[1,768,512]{2,1,0:T(8,128)}), f32[1,3072,512]{2,1,0:T(8,128)}) %all-gather.11.cloned.1.call-update) | async-done | bytes 6291472 | tf_op jit(solution)/shard_map/all_gather | solution.py:33
  133.0 66.4 %multiply_bitcast_fusion.1 = f32[3072,512]{0,1:T(8,128)} fusion(f32[3072,3072]{1,0:T(8,128)} %param.8, f32[1,3072,512]{2,1,0:T(8,128)} %all-gather.11.cloned.1.call-done, f32[3072]{0:T(1024)S(1)} %get-tuple-element.32), kind=kOutput, calls=%fused_computation.11 | convolution fusion | flops 28992602112 | bytes 50343936 | tf_op jit(solution)/shard_map/dot_general | solution.py:34
  199.5 0.0 reduce-scatter.7.cloned.1.call-start
  199.5 48.7 %all-gather.13.cloned.1.call-done = f32[1,3072,512]{2,1,0:T(8,128)} async-done(((f32[1,768,512]{2,1,0:T(8,128)}), f32[1,3072,512]{2,1,0:T(8,128)}) %all-gather.13.cloned.1.call-update) | async-done | bytes 6291472 | tf_op jit(solution)/shard_map/all_gather | solution.py:33
  248.2 66.4 %multiply_bitcast_fusion = f32[3072,512]{0,1:T(8,128)} fusion(f32[3072,3072]{1,0:T(8,128)} %param.8, f32[1,3072,512]{2,1,0:T(8,128)} %all-gather.13.cloned.1.call-done, f32[3072]{0:T(1024)S(1)} %get-tuple-element.33), kind=kOutput, calls=%fused_computation.10 | convolution fusion | flops 28992602112 | bytes 50343936 | tf_op jit(solution)/shard_map/dot_general | solution.py:34
  314.6 0.0 all-gather.7.cloned.1.call-start
  314.7 3.5 fusion.13
  318.3 53.1 %reduce-scatter.7.cloned.1.call-done = f32[3072,128]{0,1:T(8,128)} async-done(((f32[3072,512]{0,1:T(8,128)}), f32[3072,128]{0,1:T(8,128)}) %reduce-scatter.7.cloned.1.call-update) | async-done | bytes 1572880 | tf_op jit(solution)/shard_map/reduce_scatter | solution.py:37
  371.4 3.4 fusion.14
  374.8 0.0 reduce-scatter.9.cloned.1.call-start
  374.9 44.3 %all-gather.7.cloned.1.call-done = f32[3072,512]{0,1:T(8,128)} async-done(((f32[3072,128]{0,1:T(8,128)}), f32[3072,512]{0,1:T(8,128)}) %all-gather.7.cloned.1.call-update) | async-done | bytes 6291472 | tf_op jit(solution)/shard_map/all_gather | solution.py:41
  419.2 14.7 %fusion.5 = f32[512,512]{1,0:T(8,128)} fusion(f32[3072,512]{0,1:T(8,128)} %all-gather.7.cloned.1.call-done, f32[1,3072,512]{2,1,0:T(8,128)} %all-gather.11.cloned.1.call-done, f32[]{:T(128)S(6)} %convert_element_type.11), kind=kOutput, calls=%fused_computation.9 | convolution fusion | flops 4833411072 | bytes 13631492 | tf_op jit(solution)/shard_map/dot_general | solution.py:43
  434.0 33.7 %all-gather.9.cloned.1.call-done = f32[3072,512]{0,1:T(8,128)} async-done(((f32[3072,128]{0,1:T(8,128)}), f32[3072,512]{0,1:T(8,128)}) %all-gather.9.cloned.1.call-update) | async-done | bytes 6291472 | tf_op jit(solution)/shard_map/all_gather | solution.py:41
  467.6 14.6 %fusion.2 = f32[512,512]{1,0:T(8,128)} fusion(f32[3072,512]{0,1:T(8,128)} %all-gather.9.cloned.1.call-done, f32[1,3072,512]{2,1,0:T(8,128)} %all-gather.13.cloned.1.call-done, f32[]{:T(128)S(6)} %convert_element_type.11), kind=kOutput, calls=%fused_computation.5 | convolution fusion | flops 4833411072 | bytes 13631492 | tf_op jit(solution)/shard_map/dot_general | solution.py:43
  482.3 12.8 %reduce-scatter.9.cloned.1.call-done = f32[512,128]{1,0:T(8,128)} async-done(((f32[512,512]{1,0:T(8,128)}), f32[512,128]{1,0:T(8,128)}) %reduce-scatter.9.cloned.1.call-update) | async-done | bytes 262160 | tf_op jit(solution)/shard_map/reduce_scatter | solution.py:51
  495.1 28.2 %reduce-scatter.11.cloned.1.call-done = f32[512,128]{1,0:T(8,128)} async-done(((f32[512,512]{1,0:T(8,128)}), f32[512,128]{1,0:T(8,128)}) %reduce-scatter.11.cloned.1.call-update) | async-done | bytes 262160 | tf_op jit(solution)/shard_map/reduce_scatter | solution.py:51
  523.3 2.1 pad_maximum_fusion
  525.4 2.4 copy.13
  527.8 36.4 %all-reduce.3.cloned.1.call-done = (f32[1,512,128]{2,1,0:T(8,128)}, f32[1,512,128]{2,1,0:T(8,128)}) async-done(((f32[1,512,128]{2,1,0:T(8,128)}, f32[1,512,128]{2,1,0:T(8,128)}), (f32[1,512,128]{2,1,0:T(8,128)}, f32[1,512,128]{2,1,0:T(8,128)})) %all-reduce.3.cloned.1.call-update) | async-done | bytes 524304 | tf_op jit(solution)/shard_map/psum | solution.py:51
  564.2 2.0 maximum_subtract_fusion
  (24 shorter events, 0.4 us)
Async XLA Ops:
  7.2 125.8 %all-gather.11.cloned.1.call-start = ((), (), s32[]{:S(2)}) async-start(), calls=%async_computation.10 | async-start | bytes 7864320 | tf_op jit(solution)/shard_map/all_gather | solution.py:33
  12.8 2.8 copy-start.1
  12.8 3.1 copy-start
  14.8 233.4 %all-gather.13.cloned.1.call-start = ((), (), s32[]{:S(2)}) async-start(), calls=%async_computation.11 | async-start | bytes 7864320 | tf_op jit(solution)/shard_map/all_gather | solution.py:33
  15.6 299.2 %reduce-scatter.5.cloned.1.call-start = ((), (), s32[]{:S(2)}) async-start(), calls=%async_computation.4 | async-start | bytes 7864320 | tf_op jit(solution)/shard_map/reduce_scatter | solution.py:37
  199.5 171.9 %reduce-scatter.7.cloned.1.call-start = ((), (), s32[]{:S(2)}) async-start(), calls=%async_computation.5 | async-start | bytes 7864320 | tf_op jit(solution)/shard_map/reduce_scatter | solution.py:37
  314.6 104.6 %all-gather.7.cloned.1.call-start = ((), (), s32[]{:S(2)}) async-start(), calls=%async_computation.6 | async-start | bytes 7864320 | tf_op jit(solution)/shard_map/all_gather | solution.py:41
  318.2 149.4 %all-gather.9.cloned.1.call-start = ((), (), s32[]{:S(2)}) async-start(), calls=%async_computation.8 | async-start | bytes 7864320 | tf_op jit(solution)/shard_map/all_gather | solution.py:41
  374.8 120.3 %reduce-scatter.9.cloned.1.call-start = ((), (), s32[]{:S(2)}) async-start(), calls=%async_computation.7 | async-start | bytes 1310720 | tf_op jit(solution)/shard_map/reduce_scatter | solution.py:51
  433.9 89.4 %reduce-scatter.11.cloned.1.call-start = ((), (), s32[]{:S(2)}) async-start(), calls=%async_computation.9 | async-start | bytes 1310720 | tf_op jit(solution)/shard_map/reduce_scatter | solution.py:51
  482.3 81.9 %all-reduce.3.cloned.1.call-start = ((), (), s32[]{:S(2)}) async-start(), calls=%async_computation.12 | async-start | bytes 1048576 | tf_op jit(solution)/shard_map/psum | solution.py:51
Sparse Core Ops, SparseCore 0:
  14.9 118.0 all-gather.10
  134.6 113.5 all-gather.12
  250.7 56.5 reduce-scatter.4
  314.8 56.5 reduce-scatter.6
  372.8 46.3 all-gather.6
  421.2 46.3 all-gather.8
  470.1 24.9 reduce-scatter.8
  498.4 24.8 reduce-scatter.10
  525.7 38.4 all-reduce.2
where the time goes:
time: 576 us; the launch traced here: 573 us
  waiting for transfers between devices  366 us (64%)
  matrix products  162 us (28%)
  local copies, waits for them, and re-layouts  15.7 us (3%)
  other arithmetic  15 us (3%)
  between operations  14.2 us (2%)
    all_gather x2, waiting for transfers between devices, shards(): gathered = lax.all_gather(masked[supernode], 'row', axis=0, tiled=True)  156 us
    dot_general x2, matrix products, shards(): jnp.dot(sigma_anc, gathered, precision=lax.Precision.HIGH, preferred_elem...  133 us
    all_gather x2, waiting for transfers between devices, shards(): wide_rj = lax.all_gather(own_rj, 'col', axis=1, tiled=True)  78 us
    reduce_scatter x2, waiting for transfers between devices, shards(): lax.psum_scatter(partial * row_mask[supernode], 'col', scatter_dimension=...  53.1 us
    reduce_scatter x2, waiting for transfers between devices, shards(): lax.psum_scatter(update, 'col', scatter_dimension=1, tiled=True)  41 us
    psum x1, waiting for transfers between devices, shards(): lax.psum(lax.psum_scatter(update, 'col', scatter_dimension=1, tiled=True)...  36.4 us
    dot_general x2, matrix products, shards(): lax.dot_general(slab, wide_rj, (((0,), (0,)), ((), ())), precision=lax.Pr...  29.3 us
  transfers between devices with their start and end apart: 9, of which 8 were waited for; matrix products, arithmetic and copies ran while one was open for 32% of the time, Pallas kernels for 0%

commit v1 on v0

--- a/solution.py
+++ b/solution.py
@@ -30,7 +30,20 @@
     rj_list = []
     update_list = []
     for supernode in range(2):
-        gathered = lax.all_gather(masked[supernode], "row", axis=0, tiled=True)
+
+        def name_regions_here(frame):
+            device_axis = "row"
+            nd = lax.axis_size(device_axis)
+            outer = [(tick - 1, tick) for tick in range(1, nd)] + [(nd - 1, 0)]
+            before = frame
+            history = [before]
+            for _ in range(nd - 1):
+                before = lax.ppermute(before, device_axis, outer)
+                history += [before]
+            f_now = jnp.concatenate([*reversed(history)], axis=0)
+            return jnp.roll(f_now, (lax.axis_index(device_axis) + 1) * before.shape[0], axis=0)
+
+        gathered = name_regions_here(masked[supernode])
         partial = jnp.dot(
             sigma_anc, gathered, precision=lax.Precision.HIGH, preferred_element_type=jnp.float32
         )

time: 576 us -> 671 us (1.16)
  waiting for transfers between devices: 366 us -> 411 us
  other arithmetic: 15 us -> 37.9 us
  matrix products: 162 us -> 176 us
  local copies, waits for them, and re-layouts: 15.7 us -> 22.7 us
    ppermute x0 -> x6, waiting for transfers between devices: none -> 204 us  [name_regions_here(): before = lax.ppermute(before, device_axis, outer)]
    all_gather x2 -> x0, waiting for transfers between devices: 156 us -> none  [shards(): gathered = lax.all_gather(masked[supernode], 'row', axis=0, tiled=True)]
    concatenate x0 -> x2, other arithmetic: none -> 22.6 us  [name_regions_here(): jnp.roll(f_now, (lax.axis_index(device_axis) + 1) * before.shape[0], axis=0)]
    dot_general x2, matrix products: 133 us -> 146 us  [shards(): jnp.dot(sigma_anc, gathered, precision=lax.Precision.HIGH, preferred_elem...]
    unnamed x5 -> x15, local copies, waits for them, and re-layouts: 2.37 us -> 11.1 us
  transfers between devices with their start and end apart: 9 -> 13, of which waited for: 8 -> 12; matrix products, arithmetic and copies ran while one was open for 32% -> 19% of each run, Pallas kernels for 0% -> 0%
where the time goes in v1:
time: 671 us; the launch traced here: 665 us
  waiting for transfers between devices  411 us (61%)
  matrix products  176 us (26%)
  other arithmetic  37.9 us (6%)
  local copies, waits for them, and re-layouts  22.7 us (3%)
  between operations  14.7 us (2%)
    ppermute x6, waiting for transfers between devices, name_regions_here(): before = lax.ppermute(before, device_axis, outer)  204 us
    dot_general x2, matrix products, shards(): jnp.dot(sigma_anc, gathered, precision=lax.Precision.HIGH, preferred_elem...  146 us
    all_gather x2, waiting for transfers between devices, shards(): wide_rj = lax.all_gather(own_rj, 'col', axis=1, tiled=True)  78.1 us
    reduce_scatter x2, waiting for transfers between devices, shards(): lax.psum_scatter(partial * row_mask[supernode], 'col', scatter_dimension=...  51.8 us
    reduce_scatter x2, waiting for transfers between devices, shards(): lax.psum_scatter(update, 'col', scatter_dimension=1, tiled=True)  40.7 us
    psum x1, waiting for transfers between devices, shards(): lax.psum(lax.psum_scatter(update, 'col', scatter_dimension=1, tiled=True)...  36.4 us
    dot_general x2, matrix products, shards(): lax.dot_general(slab, wide_rj, (((0,), (0,)), ((), ())), precision=lax.Pr...  29.3 us
    concatenate x2, other arithmetic, name_regions_here(): jnp.roll(f_now, (lax.axis_index(device_axis) + 1) * before.shape[0], axis=0)  22.6 us
  transfers between devices with their start and end apart: 13, of which 12 were waited for; matrix products, arithmetic and copies ran while one was open for 19% of the time, Pallas kernels for 0%

profile of v1, /device:TPU:0, one launch (start us, length us, event | category | flops | bytes accessed | tf_op | source)
XLA Modules:
  0.0 665.3 jit_solution(18407191615659276135)
XLA Ops:
  8.9 1.6 gather_fusion
  10.6 2.2 broadcast_multiply_fusion
  13.1 1.2 copy-done.2
  14.3 3.0 collective-permute-start
  17.3 36.4 %collective-permute-done = f32[768,512]{1,0:T(8,128)S(1)} collective-permute-done((f32[768,512]{1,0:T(8,128)S(1)}, f32[768,512]{1,0:T(8,128)S(1)}, u32[]{:S(2)}, u32[]{:S(2)}) %collective-permute-start) | collective-permute-done | bytes 1572896 | tf_op jit(solution)/shard_map/ppermute | solution.py:41
  53.7 1.1 copy-done.3
  54.9 37.5 %collective-permute-done.1 = f32[768,512]{1,0:T(8,128)} collective-permute-done((f32[768,512]{1,0:T(8,128)S(1)}, f32[768,512]{1,0:T(8,128)}, u32[]{:S(2)}, u32[]{:S(2)}) %collective-permute-start.1) | collective-permute-done | bytes 1572896 | tf_op jit(solution)/shard_map/ppermute | solution.py:41
  92.7 8.1 %gather_fusion.1 = f32[3072,2]{1,0:T(8,128)S(1)} fusion(f32[2,64]{0,1:T(8,128)S(1)} %copy.12, s32[3072]{0:T(1024)S(1)} %broadcast_clamp_fusion), kind=kCustom, calls=%fused_computation.1 | custom fusion | bytes 61440 | tf_op jit(solution)/shard_map/jit(_take)/gather | solution.py:12
  100.8 1.3 slice_reduce_fusion.1
  102.1 27.0 %collective-permute-done.2 = f32[768,512]{1,0:T(8,128)} collective-permute-done((f32[768,512]{1,0:T(8,128)}, f32[768,512]{1,0:T(8,128)}, u32[]{:S(2)}, u32[]{:S(2)}) %collective-permute-start.2) | collective-permute-done | bytes 1572896 | tf_op jit(solution)/shard_map/ppermute | solution.py:41
  129.1 10.5 %fusion.10 = f32[3072,512]{1,0:T(8,128)S(1)} fusion(s32[]{:T(128)S(6)} %select_n.56, f32[768,512]{1,0:T(8,128)} %collective-permute-done.2, f32[768,512]{1,0:T(8,128)} %collective-permute-done.1, f32[768,512]{1,0:T(8,128)} %copy-done.3, f32[768,512]{1,0:T(8,128)} %copy-done.2), kind=kLoop, calls=%fused_computation.28 | loop fusion | flops 11010048 | bytes 12582916 | tf_op jit(solution)/shard_map/jit(_roll_dynamic)/concatenate | solution.py:44
  139.6 2.6 copy-done
  142.3 80.1 %multiply_bitcast_fusion.1 = f32[3072,512]{0,1:T(8,128)} fusion(f32[3072,512]{1,0:T(8,128)S(1)} %fusion.10, f32[3072,3072]{1,0:T(8,128)} %param.10, f32[3072]{0:T(1024)S(1)} %get-tuple-element.33), kind=kOutput, calls=%fused_computation.37 | convolution fusion | flops 28992602112 | bytes 50343936 | tf_op jit(solution)/shard_map/dot_general | solution.py:47
  222.5 35.5 %collective-permute-done.3 = f32[768,512]{1,0:T(8,128)S(1)} collective-permute-done((f32[768,512]{1,0:T(8,128)S(1)}, f32[768,512]{1,0:T(8,128)S(1)}, u32[]{:S(2)}, u32[]{:S(2)}) %collective-permute-start.3) | collective-permute-done | bytes 1572896 | tf_op jit(solution)/shard_map/ppermute | solution.py:41
  258.1 34.6 %collective-permute-done.4 = f32[768,512]{1,0:T(8,128)S(1)} collective-permute-done((f32[768,512]{1,0:T(8,128)S(1)}, f32[768,512]{1,0:T(8,128)S(1)}, u32[]{:S(2)}, u32[]{:S(2)}) %collective-permute-start.4) | collective-permute-done | bytes 1572896 | tf_op jit(solution)/shard_map/ppermute | solution.py:41
  293.8 32.7 %collective-permute-done.5 = f32[768,512]{1,0:T(8,128)} collective-permute-done((f32[768,512]{1,0:T(8,128)S(1)}, f32[768,512]{1,0:T(8,128)}, u32[]{:S(2)}, u32[]{:S(2)}) %collective-permute-start.5) | collective-permute-done | bytes 1572896 | tf_op jit(solution)/shard_map/ppermute | solution.py:41
  326.5 12.1 %fusion.3 = f32[3072,512]{1,0:T(8,128)S(1)} fusion(s32[]{:T(128)S(6)} %select_n.56, f32[768,512]{1,0:T(8,128)} %collective-permute-done.5, f32[768,512]{1,0:T(8,128)} %copy-done.4, f32[768,512]{1,0:T(8,128)S(1)} %collective-permute-done.3, f32[768,512]{1,0:T(8,128)S(1)} %get-tuple-element.38), kind=kLoop, calls=%fused_computation.21 | loop fusion | flops 11010048 | bytes 12582916 | tf_op jit(solution)/shard_map/jit(_roll_dynamic)/concatenate | solution.py:44
  338.6 2.6 copy-done.1
  341.3 66.3 %multiply_bitcast_fusion = f32[3072,512]{0,1:T(8,128)} fusion(f32[3072,512]{1,0:T(8,128)S(1)} %fusion.3, f32[3072,3072]{1,0:T(8,128)} %param.10, f32[3072]{0:T(1024)S(1)} %get-tuple-element.34), kind=kOutput, calls=%fused_computation.36 | convolution fusion | flops 28992602112 | bytes 50343936 | tf_op jit(solution)/shard_map/dot_general | solution.py:47
  407.7 3.8 fusion.20
  411.6 51.8 %reduce-scatter.7.cloned.1.call-done = f32[3072,128]{0,1:T(8,128)} async-done(((f32[3072,512]{0,1:T(8,128)}), f32[3072,128]{0,1:T(8,128)}) %reduce-scatter.7.cloned.1.call-update) | async-done | bytes 1572880 | tf_op jit(solution)/shard_map/reduce_scatter | solution.py:50
  463.4 3.4 fusion.21
  466.9 44.4 %all-gather.3.cloned.1.call-done = f32[3072,512]{0,1:T(8,128)} async-done(((f32[3072,128]{0,1:T(8,128)}), f32[3072,512]{0,1:T(8,128)}) %all-gather.3.cloned.1.call-update) | async-done | bytes 6291472 | tf_op jit(solution)/shard_map/all_gather | solution.py:54
  511.4 14.7 %fusion.16 = f32[512,512]{1,0:T(8,128)} fusion(f32[3072,512]{0,1:T(8,128)} %all-gather.3.cloned.1.call-done, f32[3072,512]{1,0:T(8,128)} %copy-done, f32[]{:T(128)S(6)} %convert_element_type.11), kind=kOutput, calls=%fused_computation.34 | convolution fusion | flops 4833411072 | bytes 13631492 | tf_op jit(solution)/shard_map/dot_general | solution.py:56
  526.1 33.6 %all-gather.5.cloned.1.call-done = f32[3072,512]{0,1:T(8,128)} async-done(((f32[3072,128]{0,1:T(8,128)}), f32[3072,512]{0,1:T(8,128)}) %all-gather.5.cloned.1.call-update) | async-done | bytes 6291472 | tf_op jit(solution)/shard_map/all_gather | solution.py:54
  559.8 14.6 %fusion.14 = f32[512,512]{1,0:T(8,128)} fusion(f32[3072,512]{0,1:T(8,128)} %all-gather.5.cloned.1.call-done, f32[3072,512]{1,0:T(8,128)} %copy-done.1, f32[]{:T(128)S(6)} %convert_element_type.11), kind=kOutput, calls=%fused_computation.32 | convolution fusion | flops 4833411072 | bytes 13631492 | tf_op jit(solution)/shard_map/dot_general | solution.py:56
  574.5 12.6 %reduce-scatter.9.cloned.1.call-done = f32[512,128]{1,0:T(8,128)} async-done(((f32[512,512]{1,0:T(8,128)}), f32[512,128]{1,0:T(8,128)}) %reduce-scatter.9.cloned.1.call-update) | async-done | bytes 262160 | tf_op jit(solution)/shard_map/reduce_scatter | solution.py:64
  587.1 28.1 %reduce-scatter.11.cloned.1.call-done = f32[512,128]{1,0:T(8,128)} async-done(((f32[512,512]{1,0:T(8,128)}), f32[512,128]{1,0:T(8,128)}) %reduce-scatter.11.cloned.1.call-update) | async-done | bytes 262160 | tf_op jit(solution)/shard_map/reduce_scatter | solution.py:64
  615.2 2.1 pad_maximum_fusion
  617.3 2.4 copy.13
  619.6 36.4 %all-reduce.3.cloned.1.call-done = (f32[1,512,128]{2,1,0:T(8,128)}, f32[1,512,128]{2,1,0:T(8,128)}) async-done(((f32[1,512,128]{2,1,0:T(8,128)}, f32[1,512,128]{2,1,0:T(8,128)}), (f32[1,512,128]{2,1,0:T(8,128)}, f32[1,512,128]{2,1,0:T(8,128)})) %all-reduce.3.cloned.1.call-update) | async-done | bytes 524304 | tf_op jit(solution)/shard_map/psum | solution.py:64
  656.1 2.0 maximum_subtract_fusion
  (42 shorter events, 4.0 us)
Async XLA Ops:
  7.2 400.5 %reduce-scatter.5.cloned.1.call-start = ((), (), s32[]{:S(2)}) async-start(), calls=%async_computation.4 | async-start | bytes 7864320 | tf_op jit(solution)/shard_map/reduce_scatter | solution.py:50
  10.6 81.8 %copy-start.6 = (s32[2,128]{1,0:T(2,128)S(1)}, s32[2,128]{1,0:T(2,128)}, u32[]{:S(2)}) copy-start(s32[2,128]{1,0:T(2,128)} %param.13) | copy-start | bytes 3076
  10.6 82.0 %copy-start.5 = (s32[3072]{0:T(1024)S(1)}, s32[3072]{0:T(1024)}, u32[]{:S(2)}) copy-start(s32[3072]{0:T(1024)} %constant.233) | copy-start | bytes 36868
  13.1 1.2 copy-start.2
  14.3 39.4 %collective-permute-start = (f32[768,512]{1,0:T(8,128)S(1)}, f32[768,512]{1,0:T(8,128)S(1)}, u32[]{:S(2)}, u32[]{:S(2)}) collective-permute-start(f32[768,512]{1,0:T(8,128)S(1)} %get-tuple-element.37), channel_id=1, source_target_pairs={{0,4},{4,8},{8,12},{12,0},{1,5},{5,9},{9,13},{13,1},{2,6},{6,10},{... | collective-permute-start | bytes 4718600 | tf_op jit(solution)/shard_map/ppermute | solution.py:41
  53.7 1.1 copy-start.3
  54.9 37.5 %collective-permute-start.1 = (f32[768,512]{1,0:T(8,128)S(1)}, f32[768,512]{1,0:T(8,128)}, u32[]{:S(2)}, u32[]{:S(2)}) collective-permute-start(f32[768,512]{1,0:T(8,128)S(1)} %collective-permute-done), channel_id=1, source_target_pairs={{0,4},{4,8},{8,12},{12,0},{1,5},{5,9},{9,13},{13,1},{2,6},{6,10},{... | collective-permute-start | bytes 4718600 | tf_op jit(solution)/shard_map/ppermute | solution.py:41
  92.3 36.8 %collective-permute-start.2 = (f32[768,512]{1,0:T(8,128)}, f32[768,512]{1,0:T(8,128)}, u32[]{:S(2)}, u32[]{:S(2)}) collective-permute-start(f32[768,512]{1,0:T(8,128)} %collective-permute-done.1), channel_id=1, source_target_pairs={{0,4},{4,8},{8,12},{12,0},{1,5},{5,9},{9,13},{13,1},{2,6},{6,10},{... | collective-permute-start | bytes 4718600 | tf_op jit(solution)/shard_map/ppermute | solution.py:41
  139.6 2.6 copy-start
  222.4 241.0 %reduce-scatter.7.cloned.1.call-start = ((), (), s32[]{:S(2)}) async-start(), calls=%async_computation.5 | async-start | bytes 7864320 | tf_op jit(solution)/shard_map/reduce_scatter | solution.py:50
  222.5 35.6 %collective-permute-start.3 = (f32[768,512]{1,0:T(8,128)S(1)}, f32[768,512]{1,0:T(8,128)S(1)}, u32[]{:S(2)}, u32[]{:S(2)}) collective-permute-start(f32[768,512]{1,0:T(8,128)S(1)} %get-tuple-element.38), channel_id=1, source_target_pairs={{0,4},{4,8},{8,12},{12,0},{1,5},{5,9},{9,13},{13,1},{2,6},{6,10},{... | collective-permute-start | bytes 4718600 | tf_op jit(solution)/shard_map/ppermute | solution.py:41
  258.1 34.6 %collective-permute-start.4 = (f32[768,512]{1,0:T(8,128)S(1)}, f32[768,512]{1,0:T(8,128)S(1)}, u32[]{:S(2)}, u32[]{:S(2)}) collective-permute-start(f32[768,512]{1,0:T(8,128)S(1)} %collective-permute-done.3), channel_id=1, source_target_pairs={{0,4},{4,8},{8,12},{12,0},{1,5},{5,9},{9,13},{13,1},{2,6},{6,10},{... | collective-permute-start | bytes 4718600 | tf_op jit(solution)/shard_map/ppermute | solution.py:41
  292.7 1.1 copy-start.4
  292.7 33.8 %collective-permute-start.5 = (f32[768,512]{1,0:T(8,128)S(1)}, f32[768,512]{1,0:T(8,128)}, u32[]{:S(2)}, u32[]{:S(2)}) collective-permute-start(f32[768,512]{1,0:T(8,128)S(1)} %collective-permute-done.4), channel_id=1, source_target_pairs={{0,4},{4,8},{8,12},{12,0},{1,5},{5,9},{9,13},{13,1},{2,6},{6,10},{... | collective-permute-start | bytes 4718600 | tf_op jit(solution)/shard_map/ppermute | solution.py:41
  338.6 2.6 copy-start.1
  407.6 103.7 %all-gather.3.cloned.1.call-start = ((), (), s32[]{:S(2)}) async-start(), calls=%async_computation.6 | async-start | bytes 7864320 | tf_op jit(solution)/shard_map/all_gather | solution.py:54
  411.5 148.3 %all-gather.5.cloned.1.call-start = ((), (), s32[]{:S(2)}) async-start(), calls=%async_computation.8 | async-start | bytes 7864320 | tf_op jit(solution)/shard_map/all_gather | solution.py:54
  466.8 120.3 %reduce-scatter.9.cloned.1.call-start = ((), (), s32[]{:S(2)}) async-start(), calls=%async_computation.7 | async-start | bytes 1310720 | tf_op jit(solution)/shard_map/reduce_scatter | solution.py:64
  526.1 89.1 %reduce-scatter.11.cloned.1.call-start = ((), (), s32[]{:S(2)}) async-start(), calls=%async_computation.9 | async-start | bytes 1310720 | tf_op jit(solution)/shard_map/reduce_scatter | solution.py:64
  574.5 81.6 %all-reduce.3.cloned.1.call-start = ((), (), s32[]{:S(2)}) async-start(), calls=%async_computation.10 | async-start | bytes 1048576 | tf_op jit(solution)/shard_map/psum | solution.py:64
Sparse Core Ops, SparseCore 0:
  222.5 56.0 reduce-scatter.4
  407.8 55.5 reduce-scatter.6
  465.0 46.3 all-gather.2
  513.4 46.3 all-gather.4
  562.1 24.9 reduce-scatter.8
  590.2 24.8 reduce-scatter.10
  617.6 38.4 all-reduce.2
